TPU v7x, 32 devices: a whole 2x2x4 slice. The times are simulated.
32 devices in a mesh: lon: 16 (over z, x, core), lat: 2 (over y).
Axes of the slice: x: 2, y: 2, z: 4, core: 2. Of those that a mesh axis runs over, the one named last changes fastest.
Arguments:
- state: float32 [5, 1, 5760, 256], P(None, None, 'lon', 'lat'), may hold values from -3 to 3
- cutoffs: int32 [2, 128], replicated, may hold values from 1 to 2879, as said below
Outputs:
- advanced: float32 [5, 1, 5760, 256], P(None, None, 'lon', 'lat')
Inputs may be any that keep to these rules, and one draw needn't show every extreme that they name: cutoffs[0, j] is the highest zonal wavenumber kept in row j and cutoffs[1, j] that of row 255 - j; in both caps the row at the pole keeps 1 and row 127 from the pole keeps 2880 - 1.
All inputs are finite; a program needn't handle non-finite values.
Results may differ from a plain program's by a relative error of at most 0.0003.
Values sent between devices are 32-bit elements; how exact they have to be, the bound alone decides.
A program may use at most 64 MiB of HBM per device.

v0:
```python
import jax
import jax.numpy as jnp
from jax import lax
from jax.sharding import PartitionSpec as P

SUBSTEPS = 2
time_step = 0.5
gravity_scale = 0.25
coriolis_scale = 0.5
wind_sign = (1.0, -1.0, -1.0, 1.0, 1.0)
highest = lax.Precision.HIGHEST
inner_factor = 64


def passed_along(value, axis, steps):
    count = lax.axis_size(axis)
    pairs = [(source, (source + steps) % count) for source in range(count)]
    return lax.ppermute(value, axis, pairs)


def extended(array, sides, width, wrap):
    for axis, dim in sides:
        peers, length = (lax.axis_size(axis), array.shape[dim])
        up = [(i, (i + 1) % peers) for i in range(peers if wrap else peers - 1)]
        down = [(j, i) for i, j in up]
        last = lax.slice_in_dim(array, length - width, length, axis=dim)
        initial = lax.slice_in_dim(array, 0, width, axis=dim)
        before = lax.ppermute(last, axis, up)
        after = lax.ppermute(initial, axis, down)
        array = jnp.concatenate([before, array, after], axis=dim)
    return array


def interface_flux(halo_padded, transported_field, advection_axis, extent_length):

    def shifted(offset):
        return lax.slice_in_dim(
            halo_padded, offset, offset + extent_length + 1, axis=advection_axis
        )

    far_west, mid_west, near_west, centre, near_east, far_east = [
        shifted(offset) for offset in range(6)
    ]
    interface_velocity = 0.5 * (
        lax.slice_in_dim(transported_field, 2, extent_length + 3, axis=advection_axis)
        + lax.slice_in_dim(transported_field, 3, extent_length + 4, axis=advection_axis)
    )
    central = (
        37.0 * (centre + near_west) - 8.0 * (near_east + mid_west) + (far_east + far_west)
    ) / 60.0
    upwind = (
        far_east - far_west - 5.0 * (near_east - mid_west) + 10.0 * (centre - near_west)
    ) / 60.0
    return interface_velocity * central - jnp.abs(interface_velocity) * upwind


def latitude_rows(first_row, row_count, total_rows):
    centres = (first_row + jnp.arange(row_count, dtype=jnp.int32)).astype(jnp.float32) + 0.5
    centre_cos = jnp.sin(centres * (jnp.pi / total_rows))
    centre_sin = -jnp.cos(centres * (jnp.pi / total_rows))
    faces = first_row + jnp.arange(row_count + 1, dtype=jnp.int32)
    face_cos = jnp.sin(
        jnp.minimum(faces, total_rows - faces).astype(jnp.float32) * (jnp.pi / total_rows)
    )
    return (centre_cos, centre_sin, face_cos)


def geopotential(fields):
    layer_mass = fields[0] * fields[3]
    return gravity_scale * jnp.flip(jnp.cumsum(jnp.flip(layer_mass, 0), axis=0), 0)


def zonal_tendency(lon_padded, centre_cos):
    lon_cells = lon_padded.shape[2] - 6
    face_fluxes = interface_flux(lon_padded, lon_padded[1:2], 2, lon_cells)
    zonal = face_fluxes[:, :, :-1] - face_fluxes[:, :, 1:]
    height = geopotential(lon_padded)
    height_slope = 0.5 * (height[:, 4 : lon_cells + 4] - height[:, 2 : lon_cells + 2])
    zonal = jnp.concatenate([zonal[:1], zonal[1:2] - height_slope[None], zonal[2:]], axis=0)
    return zonal / centre_cos


def phase_table(first, second, modulus, total):
    angle = (first[:, None] * second[None, :] % modulus).astype(jnp.float32) * (
        2.0 * jnp.pi / total
    )
    return (jnp.cos(angle), jnp.sin(angle))


def truncate_rows(rows, row_limit, lon_total):
    row_count = rows.shape[0]
    outer = lon_total // inner_factor
    outer_index = jnp.arange(outer, dtype=jnp.int32)
    inner_index = jnp.arange(inner_factor, dtype=jnp.int32)
    outer_cos, outer_sin = phase_table(outer_index, outer_index, outer, outer)
    twist_cos, twist_sin = phase_table(outer_index, inner_index, lon_total, lon_total)
    inner_cos, inner_sin = phase_table(inner_index, inner_index, inner_factor, inner_factor)
    folded = rows.reshape(row_count, outer, inner_factor)
    first_re = jnp.einsum("rpq,pk->rkq", folded, outer_cos, precision=highest)
    first_im = -jnp.einsum("rpq,pk->rkq", folded, outer_sin, precision=highest)
    turned_re = first_re * twist_cos + first_im * twist_sin
    turned_im = first_im * twist_cos - first_re * twist_sin
    spec_re = jnp.einsum("rkq,qj->rkj", turned_re, inner_cos, precision=highest) + jnp.einsum(
        "rkq,qj->rkj", turned_im, inner_sin, precision=highest
    )
    spec_im = jnp.einsum("rkq,qj->rkj", turned_im, inner_cos, precision=highest) - jnp.einsum(
        "rkq,qj->rkj", turned_re, inner_sin, precision=highest
    )
    wave = outer_index[:, None] + outer * inner_index[None, :]
    wave = jnp.minimum(wave, lon_total - wave).astype(jnp.float32)
    kept = wave[None, :, :] <= row_limit[:, None, None]
    spec_re = jnp.where(kept, spec_re, 0.0)
    spec_im = jnp.where(kept, spec_im, 0.0)
    back_re = jnp.einsum("rkj,qj->rkq", spec_re, inner_cos, precision=highest) - jnp.einsum(
        "rkj,qj->rkq", spec_im, inner_sin, precision=highest
    )
    back_im = jnp.einsum("rkj,qj->rkq", spec_re, inner_sin, precision=highest) + jnp.einsum(
        "rkj,qj->rkq", spec_im, inner_cos, precision=highest
    )
    untwist_re = back_re * twist_cos - back_im * twist_sin
    untwist_im = back_re * twist_sin + back_im * twist_cos
    result = jnp.einsum("rkq,pk->rpq", untwist_re, outer_cos, precision=highest) - jnp.einsum(
        "rkq,pk->rpq", untwist_im, outer_sin, precision=highest
    )
    return result.reshape(row_count, lon_total) / lon_total


def crossing_rims(state, is_south, is_north):
    lat_cells = state.shape[3]
    lon_count = lax.axis_size("lon")
    wind_flip = jnp.array(wind_sign, dtype=jnp.float32)[:, None, None, None]
    pole_rows = jnp.where(is_south, state[..., 0:2], state[..., lat_cells - 2 :])
    partner = passed_along(pole_rows, "lon", lon_count // 2) * wind_flip
    lat_halo = extended(state, (("lat", 3),), 3, False)
    south_rim = jnp.where(
        is_south,
        jnp.concatenate([lat_halo[..., 0:1], partner[..., 1:2], partner[..., 0:1]], axis=3),
        lat_halo[..., 0:3],
    )
    north_rim = jnp.where(
        is_north,
        jnp.concatenate(
            [partner[..., 1:2], partner[..., 0:1], lat_halo[..., lat_cells + 5 :]], axis=3
        ),
        lat_halo[..., lat_cells + 3 :],
    )
    return jnp.concatenate([south_rim, state, north_rim], axis=3)


def advance(state, geometry, cutoff_row, is_south, is_north):
    centre_cos, centre_sin, face_cos = geometry
    field_count, level_count, lon_cells, lat_cells = state.shape
    lon_count = lax.axis_size("lon")
    lon_total = lon_cells * lon_count
    lon_padded = extended(state, (("lon", 2),), 3, True)
    zonal = zonal_tendency(lon_padded, centre_cos)
    row_block = jnp.transpose(zonal, (0, 1, 3, 2)).reshape(lon_count, -1, lon_cells)
    row_limits = jnp.broadcast_to(cutoff_row, (field_count, level_count, lat_cells)).reshape(
        lon_count, -1, 1
    )
    values = lax.all_to_all(row_block, "lon", split_axis=0, concat_axis=2, tiled=True)
    limits = lax.all_to_all(row_limits, "lon", split_axis=0, concat_axis=2, tiled=True)
    spread = truncate_rows(values[0], limits[0, :, 0], lon_total)[None]
    returned = lax.all_to_all(spread, "lon", split_axis=2, concat_axis=0, tiled=True)
    filtered = jnp.transpose(
        returned.reshape(field_count, level_count, lat_cells, lon_cells), (0, 1, 3, 2)
    )
    zonal = jnp.where(jnp.logical_or(is_south, is_north), filtered, zonal)
    lat_padded = crossing_rims(state, is_south, is_north)
    merid_fluxes = interface_flux(lat_padded, lat_padded[2:3], 3, lat_cells) * face_cos
    meridional = (merid_fluxes[..., :-1] - merid_fluxes[..., 1:]) / centre_cos
    height = geopotential(lat_padded)
    north_slope = 0.5 * (height[..., 4 : lat_cells + 4] - height[..., 2 : lat_cells + 2])
    turning = coriolis_scale * centre_sin
    flux_tendency = zonal + meridional
    east_wind = flux_tendency[1] + turning * state[2]
    north_wind = flux_tendency[2] - turning * state[1] - north_slope
    flux_tendency = jnp.concatenate(
        [flux_tendency[:1], east_wind[None], north_wind[None], flux_tendency[3:]], axis=0
    )
    return state + time_step * flux_tendency


def shards(state, cutoffs):
    lat_index = lax.axis_index("lat")
    lat_count = lax.axis_size("lat")
    lat_cells = state.shape[3]
    geometry = latitude_rows(lat_index * lat_cells, lat_cells, lat_cells * lat_count)
    is_south = lat_index == 0
    is_north = lat_index == lat_count - 1
    north_row = jnp.where(is_north, jnp.flip(cutoffs[1], 0), -1)
    cutoff_row = jnp.where(is_south, cutoffs[0], north_row).astype(jnp.float32)
    for substep_index in range(SUBSTEPS):
        state = advance(state, geometry, cutoff_row, is_south, is_north)
    return state


def solution(mesh):
    return jax.shard_map(
        shards,
        mesh=mesh,
        in_specs=(P(None, None, "lon", "lat"), P()),
        out_specs=P(None, None, "lon", "lat"),
        check_vma=False,
    )
```

profile of v0, /device:TPU:9, one launch (start us, length us, event | category | flops | bytes accessed | tf_op | source)
XLA Modules:
  0.0 308.5 jit_solution(16900312575509501687)
XLA Ops:
  4.8 8.6 %all-to-all-start = ((f32[16,40,1]{1,2,0:T(1,128)}), f32[16,40,1]{1,2,0:T(1,128)S(1)}, u32[]{:S(2)}, u32[]{:S(2)}) async-start(f32[16,40,1]{1,2,0:T(1,128)} %bitcast.2), calls=%async_computation | async-start | bytes 16384 | tf_op jit(solution)/shard_map/all_to_all | solution.py:162
  18.1 5.3 %all-to-all-start.1 = ((f32[16,40,360]{2,1,0:T(8,128)}), f32[16,40,360]{2,1,0:T(8,128)S(1)}, u32[]{:S(2)}, u32[]{:S(2)}) async-start(f32[16,40,360]{2,1,0:T(8,128)} %bitcast.260), calls=%async_computation.1 | async-start | bytes 1966080 | tf_op jit(solution)/shard_map/all_to_all | solution.py:161
  26.1 2.1 collective-permute-start.2
  34.0 4.0 %collective-permute-start.4 = (f32[5,1,360,3]{2,1,3,0:T(1,128)S(1)}, f32[5,1,360,3]{2,1,3,0:T(1,128)S(1)}, u32[]{:S(2)}, u32[]{:S(2)}) collective-permute-start(f32[5,1,360,3]{2,1,3,0:T(1,128)S(1)} %copy.270), channel_id=1, source_target_pairs={{0,1},{2,3},{4,5},{6,7},{8,9},{10,11},{12,13},{14,15},{16,17},{18,... | collective-permute-start | bytes 64808 | tf_op jit(solution)/shard_map/ppermute | solution.py:28
  38.4 8.9 %all-to-all-done.1 = f32[16,40,360]{2,1,0:T(8,128)S(1)} async-done(((f32[16,40,360]{2,1,0:T(8,128)}), f32[16,40,360]{2,1,0:T(8,128)S(1)}, u32[]{:S(2)}, u32[]{:S(2)}) %all-to-all-start.1) | async-done | bytes 921632 | tf_op jit(solution)/shard_map/all_to_all | solution.py:161
  48.4 3.4 %reshape_squeeze.6 = f32[40,90,64]{2,1,0:T(8,128)} reshape(f32[1,40,16,360]{3,2,1,0:T(8,128)} %copy.204) | data formatting | bytes 1843200 | tf_op jit(solution)/shard_map/reshape;squeeze | solution.py:98
  51.8 2.1 copy.205
  56.7 1.6 fusion.18
  58.4 1.6 fusion.22
  60.0 1.8 compare_select_fusion.3
  64.6 1.8 compare_select_fusion.2
  66.4 1.8 convolution_subtract_fusion.2
  68.2 1.8 multiply_add_fusion.2
  73.1 3.6 %copy.259 = f32[40,90,64]{0,2,1:T(8,128)} copy(f32[40,90,64]{1,2,0:T(8,128)S(1)} %multiply_bitcast_fusion.1) | data formatting | bytes 1843200 | tf_op jit(solution)/shard_map/div | solution.py:125
  77.3 27.7 %reduce = f32[5760,40]{1,0:T(8,128)} reduce(f32[5760,1,40]{2,1,0:T(1,128)} %bitcast.246, f32[]{:T(128)} %broadcast.641), dimensions={1}, to_apply=%bitcast.202.reduce_sub_computation | reduce | bytes 1843204
  105.0 4.8 %reshape.638 = f32[16,1,14400]{2,1,0:T(1,128)} reshape(f32[5760,40]{1,0:T(8,128)} %reduce) | data formatting | bytes 1843200
  109.8 5.3 %all-to-all-start.2 = ((f32[16,1,14400]{2,1,0:T(1,128)}), f32[16,1,14400]{2,1,0:T(1,128)}, u32[]{:S(2)}, u32[]{:S(2)}) async-start(f32[16,1,14400]{2,1,0:T(1,128)} %reshape.638), calls=%async_computation.2 | async-start | bytes 1851392 | tf_op jit(solution)/shard_map/all_to_all | solution.py:164
  121.0 2.8 maximum_select_fusion.1
  125.2 3.6 %subtract_multiply_fusion.1 = f32[5,1,360,129]{3,2,1,0:T(8,128)S(1)} fusion(f32[5,1,360,3]{3,2,1,0:T(8,128)S(1)} %get-tuple-element.20, f32[5,1,360,128]{3,2,1,0:T(8,128)S(1)} %copy-done, f32[5,1,360,3]{3,2,1,0:T(8,128)S(1)} %get-tuple-element.19, f32[129]{0:T(256)S(1)} %fusion.173, f32[360,129]{1,0:T(8,128)S(1)} %multiply_bitcast_fusion.4, ...), kind=kLoop, calls=%fused_computation.41 | loop fusion | flops 5572800 | bytes 2265636 | tf_op jit(solution)/shard_map/mul | solution.py:170
  128.8 8.7 %all-to-all-done.2 = f32[16,1,14400]{2,1,0:T(1,128)} async-done(((f32[16,1,14400]{2,1,0:T(1,128)}), f32[16,1,14400]{2,1,0:T(1,128)}, u32[]{:S(2)}, u32[]{:S(2)}) %all-to-all-start.2) | async-done | bytes 921632 | tf_op jit(solution)/shard_map/all_to_all | solution.py:164
  137.5 4.9 %reduce.1 = f32[16,14400]{1,0:T(8,128)} reduce(f32[16,1,14400]{2,1,0:T(1,128)} %all-to-all-done.2, f32[]{:T(128)} %broadcast.641), dimensions={1}, to_apply=%all_to_all.69.reduce_sub_computation | reduce | bytes 1843204 | tf_op jit(solution)/shard_map/all_to_all | solution.py:164
  142.4 8.8 %reshape.639 = f32[5760,1,40]{2,1,0:T(1,128)} reshape(f32[16,14400]{1,0:T(8,128)} %reduce.1) | data formatting | bytes 1843200
  151.2 3.1 copy.213
  154.3 2.5 copy.214
  156.7 1.7 fusion.36
  159.8 2.1 collective-permute-start.6
  165.4 9.8 %all-to-all-start.3 = ((f32[16,40,360]{2,1,0:T(8,128)}), f32[16,40,360]{2,1,0:T(8,128)S(1)}, u32[]{:S(2)}, u32[]{:S(2)}) async-start(f32[16,40,360]{2,1,0:T(8,128)} %bitcast.261), calls=%async_computation.3 | async-start | bytes 1966080 | tf_op jit(solution)/shard_map/all_to_all | solution.py:161
  181.0 4.0 %collective-permute-start.9 = (f32[5,1,360,3]{2,1,3,0:T(1,128)S(1)}, f32[5,1,360,3]{2,1,3,0:T(1,128)S(1)}, u32[]{:S(2)}, u32[]{:S(2)}) collective-permute-start(f32[5,1,360,3]{2,1,3,0:T(1,128)S(1)} %copy.244), channel_id=1, source_target_pairs={{0,1},{2,3},{4,5},{6,7},{8,9},{10,11},{12,13},{14,15},{16,17},{18,... | collective-permute-start | bytes 64808 | tf_op jit(solution)/shard_map/ppermute | solution.py:28
  187.8 2.2 collective-permute-start.7
  190.0 9.3 %all-to-all-done.3 = f32[16,40,360]{2,1,0:T(8,128)S(1)} async-done(((f32[16,40,360]{2,1,0:T(8,128)}), f32[16,40,360]{2,1,0:T(8,128)S(1)}, u32[]{:S(2)}, u32[]{:S(2)}) %all-to-all-start.3) | async-done | bytes 921632 | tf_op jit(solution)/shard_map/all_to_all | solution.py:161
  200.3 3.4 %reshape_squeeze.7 = f32[40,90,64]{2,1,0:T(8,128)} reshape(f32[1,40,16,360]{3,2,1,0:T(8,128)} %copy.226) | data formatting | bytes 1843200 | tf_op jit(solution)/shard_map/reshape;squeeze | solution.py:98
  203.7 1.9 copy.227
  208.4 1.6 fusion.12
  210.1 1.6 fusion.16
  211.7 1.8 compare_select_fusion.1
  216.3 1.8 compare_select_fusion
  219.7 1.8 multiply_add_fusion
  224.6 3.6 %copy.264 = f32[40,90,64]{0,2,1:T(8,128)} copy(f32[40,90,64]{1,2,0:T(8,128)S(1)} %multiply_bitcast_fusion) | data formatting | bytes 1843200 | tf_op jit(solution)/shard_map/div | solution.py:125
  228.2 27.7 %reduce.2 = f32[5760,40]{1,0:T(8,128)} reduce(f32[5760,1,40]{2,1,0:T(1,128)} %bitcast.248, f32[]{:T(128)} %broadcast.641), dimensions={1}, to_apply=%bitcast.204.reduce_sub_computation | reduce | bytes 1843204
  255.9 4.8 %reshape.640 = f32[16,1,14400]{2,1,0:T(1,128)} reshape(f32[5760,40]{1,0:T(8,128)} %reduce.2) | data formatting | bytes 1843200
  260.7 5.1 %all-to-all-start.4 = ((f32[16,1,14400]{2,1,0:T(1,128)}), f32[16,1,14400]{2,1,0:T(1,128)S(1)}, u32[]{:S(2)}, u32[]{:S(2)}) async-start(f32[16,1,14400]{2,1,0:T(1,128)} %reshape.640), calls=%async_computation.4 | async-start | bytes 1851392 | tf_op jit(solution)/shard_map/all_to_all | solution.py:164
  273.6 3.9 %maximum_select_fusion.3 = (f32[5,1,360,3]{3,2,1,0:T(8,128)S(1)}, f32[5,1,360,3]{3,2,1,0:T(8,128)S(1)}) fusion(f32[5,1,360,3]{3,2,1,0:T(8,128)} %copy.246, f32[5,1,360,1]{3,2,1,0:T(8,128)} %copy.272, f32[5,1,360,1]{3,2,1,0:T(8,128)} %copy.271, f32[5,1,360,1]{3,2,1,0:T(8,128)} %copy.245, pred[]{:T(512)S(6)} %eq.15, f32[5,1,360,3]{3,2,1,0:T(8,128)} %copy.243, ...), kind=kLoop, calls=%fused_computation.108 | loop fusion | flops 32400 | bytes 115202 | tf_op jit(solution)/shard_map/jit(_where)/select_n | solution.py:135
  278.1 4.5 %subtract_multiply_fusion = f32[5,1,360,129]{3,2,1,0:T(8,128)} fusion(f32[5,1,360,3]{3,2,1,0:T(8,128)S(1)} %get-tuple-element.18, f32[5,1,360,128]{3,2,1,0:T(8,128)S(1)} %fusion.37, f32[5,1,360,3]{3,2,1,0:T(8,128)S(1)} %get-tuple-element.17, f32[360,129]{1,0:T(8,128)S(1)} %multiply_bitcast_fusion.2, f32[360,129]{1,0:T(8,128)S(1)} %get-tuple-element.7, ...), kind=kLoop, calls=%fused_computation.40 | loop fusion | flops 5572800 | bytes 2265636 | tf_op jit(solution)/shard_map/mul | solution.py:170
  282.7 5.5 %all-to-all-done.4 = f32[16,1,14400]{2,1,0:T(1,128)S(1)} async-done(((f32[16,1,14400]{2,1,0:T(1,128)}), f32[16,1,14400]{2,1,0:T(1,128)S(1)}, u32[]{:S(2)}, u32[]{:S(2)}) %all-to-all-start.4) | async-done | bytes 921632 | tf_op jit(solution)/shard_map/all_to_all | solution.py:164
  288.2 4.1 %reduce.3 = f32[16,14400]{1,0:T(8,128)} reduce(f32[16,1,14400]{2,1,0:T(1,128)S(1)} %all-to-all-done.4, f32[]{:T(128)} %broadcast.641), dimensions={1}, to_apply=%all_to_all.75.reduce_sub_computation | reduce | bytes 1843204 | tf_op jit(solution)/shard_map/all_to_all | solution.py:164
  292.2 8.8 %reshape.641 = f32[5760,1,40]{2,1,0:T(1,128)} reshape(f32[16,14400]{1,0:T(8,128)} %reduce.3) | data formatting | bytes 1843200
  301.0 2.3 copy.235
  304.5 2.4 fusion.34
  (122 shorter events, 71.7 us)
Async XLA Ops:
  0.0 14.7 %copy-start = (f32[5,1,360,128]{3,2,1,0:T(8,128)S(1)}, f32[5,1,360,128]{3,2,1,0:T(8,128)}, u32[]{:S(2)}) copy-start(f32[5,1,360,128]{3,2,1,0:T(8,128)} %param.4) | copy-start | bytes 2764804
  0.8 13.9 %collective-permute-start = (f32[5,1,3,128]{3,2,1,0:T(4,128)S(1)}, f32[5,1,3,128]{3,2,1,0:T(4,128)S(1)}, u32[]{:S(2)}, u32[]{:S(2)}) collective-permute-start(f32[5,1,3,128]{3,2,1,0:T(4,128)S(1)} %get-tuple-element.33), channel_id=1, source_target_pairs={{2,0},{4,2},{6,4},{8,6},{10,8},{12,10},{14,12},{16,14},{18,16},{20... | collective-permute-start | bytes 23048 | tf_op jit(solution)/shard_map/ppermute | solution.py:29
  1.5 13.2 %collective-permute-start.1 = (f32[5,1,3,128]{3,2,1,0:T(4,128)S(1)}, f32[5,1,3,128]{3,2,1,0:T(4,128)S(1)}, u32[]{:S(2)}, u32[]{:S(2)}) collective-permute-start(f32[5,1,3,128]{3,2,1,0:T(4,128)S(1)} %get-tuple-element.34), channel_id=1, source_target_pairs={{0,2},{2,4},{4,6},{6,8},{8,10},{10,12},{12,14},{14,16},{16,18},{18... | collective-permute-start | bytes 23048 | tf_op jit(solution)/shard_map/ppermute | solution.py:28
  4.8 13.3 %all-to-all-start = ((f32[16,40,1]{1,2,0:T(1,128)}), f32[16,40,1]{1,2,0:T(1,128)S(1)}, u32[]{:S(2)}, u32[]{:S(2)}) async-start(f32[16,40,1]{1,2,0:T(1,128)} %bitcast.2), calls=%async_computation | async-start | bytes 16384 | tf_op jit(solution)/shard_map/all_to_all | solution.py:162
  15.9 1.4 copy-start.1
  15.9 1.4 copy-start.2
  18.1 29.2 %all-to-all-start.1 = ((f32[16,40,360]{2,1,0:T(8,128)}), f32[16,40,360]{2,1,0:T(8,128)S(1)}, u32[]{:S(2)}, u32[]{:S(2)}) async-start(f32[16,40,360]{2,1,0:T(8,128)} %bitcast.260), calls=%async_computation.1 | async-start | bytes 1966080 | tf_op jit(solution)/shard_map/all_to_all | solution.py:161
  26.1 89.0 %collective-permute-start.2 = (f32[5,1,360,2]{2,3,1,0:T(2,128)S(1)}, f32[5,1,360,2]{2,3,1,0:T(2,128)S(1)}, u32[]{:S(2)}, u32[]{:S(2)}) collective-permute-start(f32[5,1,360,2]{2,3,1,0:T(2,128)S(1)} %copy.215), channel_id=1, source_target_pairs={{0,16},{2,18},{4,20},{6,22},{8,24},{10,26},{12,28},{14,30},{16,0},... | collective-permute-start | bytes 43208 | tf_op jit(solution)/shard_map/ppermute | solution.py:18
  31.2 84.6 %collective-permute-start.3 = (f32[5,1,360,3]{2,1,3,0:T(1,128)S(1)}, f32[5,1,360,3]{2,1,3,0:T(1,128)S(1)}, u32[]{:S(2)}, u32[]{:S(2)}) collective-permute-start(f32[5,1,360,3]{2,1,3,0:T(1,128)S(1)} %copy.269), channel_id=1, source_target_pairs={{1,0},{3,2},{5,4},{7,6},{9,8},{11,10},{13,12},{15,14},{17,16},{19,... | collective-permute-start | bytes 64808 | tf_op jit(solution)/shard_map/ppermute | solution.py:29
  34.0 83.1 %collective-permute-start.4 = (f32[5,1,360,3]{2,1,3,0:T(1,128)S(1)}, f32[5,1,360,3]{2,1,3,0:T(1,128)S(1)}, u32[]{:S(2)}, u32[]{:S(2)}) collective-permute-start(f32[5,1,360,3]{2,1,3,0:T(1,128)S(1)} %copy.270), channel_id=1, source_target_pairs={{0,1},{2,3},{4,5},{6,7},{8,9},{10,11},{12,13},{14,15},{16,17},{18,... | collective-permute-start | bytes 64808 | tf_op jit(solution)/shard_map/ppermute | solution.py:28
  109.8 5.3 %copy-start.4 = (f32[5]{0:T(128)S(1)}, f32[5]{0:T(128)}, u32[]{:S(2)}) copy-start(f32[5]{0:T(128)} %constant.123.clone) | copy-start | bytes 64
  109.8 27.7 %all-to-all-start.2 = ((f32[16,1,14400]{2,1,0:T(1,128)}), f32[16,1,14400]{2,1,0:T(1,128)}, u32[]{:S(2)}, u32[]{:S(2)}) async-start(f32[16,1,14400]{2,1,0:T(1,128)} %reshape.638), calls=%async_computation.2 | async-start | bytes 1851392 | tf_op jit(solution)/shard_map/all_to_all | solution.py:164
  158.4 1.0 copy-start.3
  159.7 3.2 %collective-permute-start.5 = (f32[5,1,3,128]{3,2,1,0:T(4,128)S(1)}, f32[5,1,3,128]{3,2,1,0:T(4,128)S(1)}, u32[]{:S(2)}, u32[]{:S(2)}) collective-permute-start(f32[5,1,3,128]{3,2,1,0:T(4,128)S(1)} %get-tuple-element.26), channel_id=1, source_target_pairs={{2,0},{4,2},{6,4},{8,6},{10,8},{12,10},{14,12},{16,14},{18,16},{20... | collective-permute-start | bytes 23048 | tf_op jit(solution)/shard_map/ppermute | solution.py:29
  159.8 3.1 %collective-permute-start.6 = (f32[5,1,3,128]{3,2,1,0:T(4,128)S(1)}, f32[5,1,3,128]{3,2,1,0:T(4,128)S(1)}, u32[]{:S(2)}, u32[]{:S(2)}) collective-permute-start(f32[5,1,3,128]{3,2,1,0:T(4,128)S(1)} %get-tuple-element.25), channel_id=1, source_target_pairs={{0,2},{2,4},{4,6},{6,8},{8,10},{10,12},{12,14},{14,16},{16,18},{18... | collective-permute-start | bytes 23048 | tf_op jit(solution)/shard_map/ppermute | solution.py:28
  165.4 33.8 %all-to-all-start.3 = ((f32[16,40,360]{2,1,0:T(8,128)}), f32[16,40,360]{2,1,0:T(8,128)S(1)}, u32[]{:S(2)}, u32[]{:S(2)}) async-start(f32[16,40,360]{2,1,0:T(8,128)} %bitcast.261), calls=%async_computation.3 | async-start | bytes 1966080 | tf_op jit(solution)/shard_map/all_to_all | solution.py:161
  178.2 90.2 %collective-permute-start.8 = (f32[5,1,360,3]{2,1,3,0:T(1,128)S(1)}, f32[5,1,360,3]{2,1,3,0:T(1,128)S(1)}, u32[]{:S(2)}, u32[]{:S(2)}) collective-permute-start(f32[5,1,360,3]{2,1,3,0:T(1,128)S(1)} %copy.241), channel_id=1, source_target_pairs={{1,0},{3,2},{5,4},{7,6},{9,8},{11,10},{13,12},{15,14},{17,16},{19,... | collective-permute-start | bytes 64808 | tf_op jit(solution)/shard_map/ppermute | solution.py:29
  181.0 88.7 %collective-permute-start.9 = (f32[5,1,360,3]{2,1,3,0:T(1,128)S(1)}, f32[5,1,360,3]{2,1,3,0:T(1,128)S(1)}, u32[]{:S(2)}, u32[]{:S(2)}) collective-permute-start(f32[5,1,360,3]{2,1,3,0:T(1,128)S(1)} %copy.244), channel_id=1, source_target_pairs={{0,1},{2,3},{4,5},{6,7},{8,9},{10,11},{12,13},{14,15},{16,17},{18,... | collective-permute-start | bytes 64808 | tf_op jit(solution)/shard_map/ppermute | solution.py:28
  187.8 78.0 %collective-permute-start.7 = (f32[5,1,360,2]{2,3,1,0:T(2,128)S(1)}, f32[5,1,360,2]{2,3,1,0:T(2,128)S(1)}, u32[]{:S(2)}, u32[]{:S(2)}) collective-permute-start(f32[5,1,360,2]{2,3,1,0:T(2,128)S(1)} %copy.237), channel_id=1, source_target_pairs={{0,16},{2,18},{4,20},{6,22},{8,24},{10,26},{12,28},{14,30},{16,0},... | collective-permute-start | bytes 43208 | tf_op jit(solution)/shard_map/ppermute | solution.py:18
  260.7 27.5 %all-to-all-start.4 = ((f32[16,1,14400]{2,1,0:T(1,128)}), f32[16,1,14400]{2,1,0:T(1,128)S(1)}, u32[]{:S(2)}, u32[]{:S(2)}) async-start(f32[16,1,14400]{2,1,0:T(1,128)} %reshape.640), calls=%async_computation.4 | async-start | bytes 1851392 | tf_op jit(solution)/shard_map/all_to_all | solution.py:164
where the time goes:
time: 314 us; the launch traced here: 308 us
  other arithmetic  93.3 us (30%)
  local copies, waits for them, and re-layouts  89.5 us (29%)
  starting transfers between devices  53 us (17%)
  matrix products  37.6 us (12%)
  waiting for transfers between devices  34.1 us (11%)
    unnamed x2, other arithmetic  55.4 us
    unnamed x22, local copies, waits for them, and re-layouts  36.1 us
    all_to_all x2, waiting for transfers between devices, advance(): lax.all_to_all(row_block, 'lon', split_axis=0, concat_axis=2, tiled=True)  18.2 us
    all_to_all x2, starting transfers between devices, advance(): lax.all_to_all(row_block, 'lon', split_axis=0, concat_axis=2, tiled=True)  15.1 us
    all_to_all x2, waiting for transfers between devices, advance(): lax.all_to_all(spread, 'lon', split_axis=2, concat_axis=0, tiled=True)  14.2 us
    unnamed x8, matrix products  11.3 us
    ppermute x4, starting transfers between devices, extended(): before = lax.ppermute(last, axis, up)  11.3 us
    another operation x4, local copies, waits for them, and re-layouts, truncate_rows(): folded = rows.reshape(row_count, outer, inner_factor)  10.7 us
  transfers between devices with their start and end apart: 15, of which 6 were waited for; matrix products, arithmetic and copies ran while one was open for 57% of the time, Pallas kernels for 0%

commit v1 on v0

--- a/solution.py
+++ b/solution.py
@@ -158,7 +158,10 @@
     row_limits = jnp.broadcast_to(cutoff_row, (field_count, level_count, lat_cells)).reshape(
         lon_count, -1, 1
     )
-    values = lax.all_to_all(row_block, "lon", split_axis=0, concat_axis=2, tiled=True)
+    values = jnp.concatenate(
+        lax.all_to_all(jnp.stack(jnp.split(row_block, lax.axis_size("lon"), axis=0)), "lon", 0, 0),
+        2,
+    )
     limits = lax.all_to_all(row_limits, "lon", split_axis=0, concat_axis=2, tiled=True)
     spread = truncate_rows(values[0], limits[0, :, 0], lon_total)[None]
     returned = lax.all_to_all(spread, "lon", split_axis=2, concat_axis=0, tiled=True)

time: 314 us -> 338 us (1.076)
  local copies, waits for them, and re-layouts: 89.5 us -> 111 us
    unnamed x22 -> x52, local copies, waits for them, and re-layouts: 36.1 us -> 55.6 us
  transfers between devices with their start and end apart: 15 -> 15, of which waited for: 6 -> 5; matrix products, arithmetic and copies ran while one was open for 57% -> 56% of each run, Pallas kernels for 0% -> 0%
where the time goes in v1:
time: 338 us; the launch traced here: 332 us
  local copies, waits for them, and re-layouts  111 us (33%)
  other arithmetic  95.2 us (28%)
  starting transfers between devices  53.8 us (16%)
  matrix products  37.6 us (11%)
  waiting for transfers between devices  33.4 us (10%)
    unnamed x52, local copies, waits for them, and re-layouts  55.6 us
    unnamed x2, other arithmetic  55.4 us
    all_to_all x2, waiting for transfers between devices, advance(): lax.all_to_all(jnp.stack(jnp.split(row_block, lax.axis_size('lon'), axis=...  18.2 us
    all_to_all x2, starting transfers between devices, advance(): lax.all_to_all(jnp.stack(jnp.split(row_block, lax.axis_size('lon'), axis=...  15.8 us
    all_to_all x2, waiting for transfers between devices, advance(): lax.all_to_all(spread, 'lon', split_axis=2, concat_axis=0, tiled=True)  14.2 us
    unnamed x8, matrix products  11.4 us
    ppermute x4, starting transfers between devices, extended(): before = lax.ppermute(last, axis, up)  11.3 us
    another operation x4, local copies, waits for them, and re-layouts, truncate_rows(): folded = rows.reshape(row_count, outer, inner_factor)  10.7 us
  transfers between devices with their start and end apart: 15, of which 5 were waited for; matrix products, arithmetic and copies ran while one was open for 56% of the time, Pallas kernels for 0%

profile of v1, /device:TPU:9, one launch (start us, length us, event | category | flops | bytes accessed | tf_op | source)
XLA Modules:
  0.0 331.5 jit_solution(1688831620994593087)
XLA Ops:
  4.8 8.6 %all-to-all-start = ((f32[16,40,1]{1,2,0:T(1,128)}), f32[16,40,1]{1,2,0:T(1,128)S(1)}, u32[]{:S(2)}, u32[]{:S(2)}) async-start(f32[16,40,1]{1,2,0:T(1,128)} %bitcast.2), calls=%async_computation | async-start | bytes 16384 | tf_op jit(solution)/shard_map/all_to_all | solution.py:165
  29.2 6.0 %all-to-all-start.1 = ((f32[16,1,40,360]{3,2,1,0:T(8,128)}), f32[16,1,40,360]{3,2,1,0:T(8,128)S(1)}, u32[]{:S(2)}, u32[]{:S(2)}) async-start(f32[16,1,40,360]{3,2,1,0:T(8,128)} %constant_dynamic-update-slice_fusion.2), calls=%async_computation.1 | async-start | bytes 1966080 | tf_op jit(solution)/shard_map/all_to_all | solution.py:162
  37.9 2.1 collective-permute-start.2
  45.9 4.0 %collective-permute-start.4 = (f32[5,1,360,3]{2,1,3,0:T(1,128)S(1)}, f32[5,1,360,3]{2,1,3,0:T(1,128)S(1)}, u32[]{:S(2)}, u32[]{:S(2)}) collective-permute-start(f32[5,1,360,3]{2,1,3,0:T(1,128)S(1)} %copy.270), channel_id=1, source_target_pairs={{0,1},{2,3},{4,5},{6,7},{8,9},{10,11},{12,13},{14,15},{16,17},{18,... | collective-permute-start | bytes 64808 | tf_op jit(solution)/shard_map/ppermute | solution.py:28
  50.2 9.0 %all-to-all-done.1 = f32[16,1,40,360]{3,2,1,0:T(8,128)S(1)} async-done(((f32[16,1,40,360]{3,2,1,0:T(8,128)}), f32[16,1,40,360]{3,2,1,0:T(8,128)S(1)}, u32[]{:S(2)}, u32[]{:S(2)}) %all-to-all-start.1) | async-done | bytes 921632 | tf_op jit(solution)/shard_map/all_to_all | solution.py:162
  60.3 3.4 %reshape_squeeze_reshape.6 = f32[40,90,64]{2,1,0:T(8,128)} reshape(f32[1,40,16,360]{3,2,1,0:T(8,128)} %copy.204) | data formatting | bytes 1843200 | tf_op jit(solution)/shard_map/reshape;squeeze;reshape | solution.py:98
  63.7 2.1 copy.205
  68.6 1.6 fusion.18
  70.2 1.6 fusion.22
  71.9 1.8 compare_select_fusion.3
  76.5 1.8 compare_select_fusion.2
  78.2 1.8 convolution_subtract_fusion.2
  80.1 1.8 multiply_add_fusion.2
  85.0 3.6 %copy.259 = f32[40,90,64]{0,2,1:T(8,128)} copy(f32[40,90,64]{1,2,0:T(8,128)S(1)} %multiply_bitcast_fusion.1) | data formatting | bytes 1843200 | tf_op jit(solution)/shard_map/div | solution.py:125
  89.1 27.7 %reduce = f32[5760,40]{1,0:T(8,128)} reduce(f32[5760,1,40]{2,1,0:T(1,128)} %bitcast.370, f32[]{:T(128)} %broadcast.641), dimensions={1}, to_apply=%bitcast.326.reduce_sub_computation | reduce | bytes 1843204
  116.8 4.8 %reshape.644 = f32[16,1,14400]{2,1,0:T(1,128)} reshape(f32[5760,40]{1,0:T(8,128)} %reduce) | data formatting | bytes 1843200
  121.6 5.3 %all-to-all-start.2 = ((f32[16,1,14400]{2,1,0:T(1,128)}), f32[16,1,14400]{2,1,0:T(1,128)}, u32[]{:S(2)}, u32[]{:S(2)}) async-start(f32[16,1,14400]{2,1,0:T(1,128)} %reshape.644), calls=%async_computation.2 | async-start | bytes 1851392 | tf_op jit(solution)/shard_map/all_to_all | solution.py:167
  132.9 2.8 maximum_select_fusion.1
  137.0 3.6 %subtract_multiply_fusion.1 = f32[5,1,360,129]{3,2,1,0:T(8,128)S(1)} fusion(f32[5,1,360,3]{3,2,1,0:T(8,128)S(1)} %get-tuple-element.20, f32[5,1,360,128]{3,2,1,0:T(8,128)S(1)} %copy-done, f32[5,1,360,3]{3,2,1,0:T(8,128)S(1)} %get-tuple-element.19, f32[129]{0:T(256)S(1)} %fusion.173, f32[360,129]{1,0:T(8,128)S(1)} %multiply_bitcast_fusion.4, ...), kind=kLoop, calls=%fused_computation.41 | loop fusion | flops 5572800 | bytes 2265636 | tf_op jit(solution)/shard_map/mul | solution.py:173
  140.6 8.7 %all-to-all-done.2 = f32[16,1,14400]{2,1,0:T(1,128)} async-done(((f32[16,1,14400]{2,1,0:T(1,128)}), f32[16,1,14400]{2,1,0:T(1,128)}, u32[]{:S(2)}, u32[]{:S(2)}) %all-to-all-start.2) | async-done | bytes 921632 | tf_op jit(solution)/shard_map/all_to_all | solution.py:167
  149.3 4.9 %reduce.1 = f32[16,14400]{1,0:T(8,128)} reduce(f32[16,1,14400]{2,1,0:T(1,128)} %all-to-all-done.2, f32[]{:T(128)} %broadcast.641), dimensions={1}, to_apply=%all_to_all.51.reduce_sub_computation | reduce | bytes 1843204 | tf_op jit(solution)/shard_map/all_to_all | solution.py:167
  154.3 8.8 %reshape.645 = f32[5760,1,40]{2,1,0:T(1,128)} reshape(f32[16,14400]{1,0:T(8,128)} %reduce.1) | data formatting | bytes 1843200
  163.0 3.1 copy.213
  166.1 2.5 copy.214
  168.6 1.7 fusion.36
  171.6 2.1 collective-permute-start.6
  188.5 9.8 %all-to-all-start.3 = ((f32[16,1,40,360]{3,2,1,0:T(8,128)}), f32[16,1,40,360]{3,2,1,0:T(8,128)S(1)}, u32[]{:S(2)}, u32[]{:S(2)}) async-start(f32[16,1,40,360]{3,2,1,0:T(8,128)} %constant_dynamic-update-slice_fusion.18), calls=%async_computation.3 | async-start | bytes 1966080 | tf_op jit(solution)/shard_map/all_to_all | solution.py:162
  204.1 4.0 %collective-permute-start.9 = (f32[5,1,360,3]{2,1,3,0:T(1,128)S(1)}, f32[5,1,360,3]{2,1,3,0:T(1,128)S(1)}, u32[]{:S(2)}, u32[]{:S(2)}) collective-permute-start(f32[5,1,360,3]{2,1,3,0:T(1,128)S(1)} %copy.244), channel_id=1, source_target_pairs={{0,1},{2,3},{4,5},{6,7},{8,9},{10,11},{12,13},{14,15},{16,17},{18,... | collective-permute-start | bytes 64808 | tf_op jit(solution)/shard_map/ppermute | solution.py:28
  210.8 2.2 collective-permute-start.7
  213.0 9.3 %all-to-all-done.3 = f32[16,1,40,360]{3,2,1,0:T(8,128)S(1)} async-done(((f32[16,1,40,360]{3,2,1,0:T(8,128)}), f32[16,1,40,360]{3,2,1,0:T(8,128)S(1)}, u32[]{:S(2)}, u32[]{:S(2)}) %all-to-all-start.3) | async-done | bytes 921632 | tf_op jit(solution)/shard_map/all_to_all | solution.py:162
  223.4 3.4 %reshape_squeeze_reshape.7 = f32[40,90,64]{2,1,0:T(8,128)} reshape(f32[1,40,16,360]{3,2,1,0:T(8,128)} %copy.226) | data formatting | bytes 1843200 | tf_op jit(solution)/shard_map/reshape;squeeze;reshape | solution.py:98
  226.8 1.9 copy.227
  231.5 1.6 fusion.12
  233.1 1.6 fusion.16
  234.8 1.8 compare_select_fusion.1
  239.4 1.8 compare_select_fusion
  242.8 1.8 multiply_add_fusion
  247.7 3.6 %copy.264 = f32[40,90,64]{0,2,1:T(8,128)} copy(f32[40,90,64]{1,2,0:T(8,128)S(1)} %multiply_bitcast_fusion) | data formatting | bytes 1843200 | tf_op jit(solution)/shard_map/div | solution.py:125
  251.3 27.7 %reduce.2 = f32[5760,40]{1,0:T(8,128)} reduce(f32[5760,1,40]{2,1,0:T(1,128)} %bitcast.372, f32[]{:T(128)} %broadcast.641), dimensions={1}, to_apply=%bitcast.328.reduce_sub_computation | reduce | bytes 1843204
  279.0 4.8 %reshape.646 = f32[16,1,14400]{2,1,0:T(1,128)} reshape(f32[5760,40]{1,0:T(8,128)} %reduce.2) | data formatting | bytes 1843200
  283.8 5.1 %all-to-all-start.4 = ((f32[16,1,14400]{2,1,0:T(1,128)}), f32[16,1,14400]{2,1,0:T(1,128)S(1)}, u32[]{:S(2)}, u32[]{:S(2)}) async-start(f32[16,1,14400]{2,1,0:T(1,128)} %reshape.646), calls=%async_computation.4 | async-start | bytes 1851392 | tf_op jit(solution)/shard_map/all_to_all | solution.py:167
  296.7 3.9 %maximum_select_fusion.3 = (f32[5,1,360,3]{3,2,1,0:T(8,128)S(1)}, f32[5,1,360,3]{3,2,1,0:T(8,128)S(1)}) fusion(f32[5,1,360,3]{3,2,1,0:T(8,128)} %copy.246, f32[5,1,360,1]{3,2,1,0:T(8,128)} %copy.272, f32[5,1,360,1]{3,2,1,0:T(8,128)} %copy.271, f32[5,1,360,1]{3,2,1,0:T(8,128)} %copy.245, pred[]{:T(512)S(6)} %eq.15, f32[5,1,360,3]{3,2,1,0:T(8,128)} %copy.243, ...), kind=kLoop, calls=%fused_computation.108 | loop fusion | flops 32400 | bytes 115202 | tf_op jit(solution)/shard_map/jit(_where)/select_n | solution.py:135
  301.2 4.5 %subtract_multiply_fusion = f32[5,1,360,129]{3,2,1,0:T(8,128)} fusion(f32[5,1,360,3]{3,2,1,0:T(8,128)S(1)} %get-tuple-element.18, f32[5,1,360,128]{3,2,1,0:T(8,128)S(1)} %fusion.37, f32[5,1,360,3]{3,2,1,0:T(8,128)S(1)} %get-tuple-element.17, f32[360,129]{1,0:T(8,128)S(1)} %multiply_bitcast_fusion.2, f32[360,129]{1,0:T(8,128)S(1)} %get-tuple-element.7, ...), kind=kLoop, calls=%fused_computation.40 | loop fusion | flops 5572800 | bytes 2265636 | tf_op jit(solution)/shard_map/mul | solution.py:173
  305.7 5.5 %all-to-all-done.4 = f32[16,1,14400]{2,1,0:T(1,128)S(1)} async-done(((f32[16,1,14400]{2,1,0:T(1,128)}), f32[16,1,14400]{2,1,0:T(1,128)S(1)}, u32[]{:S(2)}, u32[]{:S(2)}) %all-to-all-start.4) | async-done | bytes 921632 | tf_op jit(solution)/shard_map/all_to_all | solution.py:167
  311.2 4.1 %reduce.3 = f32[16,14400]{1,0:T(8,128)} reduce(f32[16,1,14400]{2,1,0:T(1,128)S(1)} %all-to-all-done.4, f32[]{:T(128)} %broadcast.641), dimensions={1}, to_apply=%all_to_all.55.reduce_sub_computation | reduce | bytes 1843204 | tf_op jit(solution)/shard_map/all_to_all | solution.py:167
  315.3 8.8 %reshape.647 = f32[5760,1,40]{2,1,0:T(1,128)} reshape(f32[16,14400]{1,0:T(8,128)} %reduce.3) | data formatting | bytes 1843200
  324.1 2.3 copy.235
  327.6 2.4 fusion.34
  (154 shorter events, 94.0 us)
Async XLA Ops:
  0.0 14.7 %copy-start = (f32[5,1,360,128]{3,2,1,0:T(8,128)S(1)}, f32[5,1,360,128]{3,2,1,0:T(8,128)}, u32[]{:S(2)}) copy-start(f32[5,1,360,128]{3,2,1,0:T(8,128)} %param.4) | copy-start | bytes 2764804
  0.8 13.9 %collective-permute-start = (f32[5,1,3,128]{3,2,1,0:T(4,128)S(1)}, f32[5,1,3,128]{3,2,1,0:T(4,128)S(1)}, u32[]{:S(2)}, u32[]{:S(2)}) collective-permute-start(f32[5,1,3,128]{3,2,1,0:T(4,128)S(1)} %get-tuple-element.33), channel_id=1, source_target_pairs={{2,0},{4,2},{6,4},{8,6},{10,8},{12,10},{14,12},{16,14},{18,16},{20... | collective-permute-start | bytes 23048 | tf_op jit(solution)/shard_map/ppermute | solution.py:29
  1.5 13.2 %collective-permute-start.1 = (f32[5,1,3,128]{3,2,1,0:T(4,128)S(1)}, f32[5,1,3,128]{3,2,1,0:T(4,128)S(1)}, u32[]{:S(2)}, u32[]{:S(2)}) collective-permute-start(f32[5,1,3,128]{3,2,1,0:T(4,128)S(1)} %get-tuple-element.34), channel_id=1, source_target_pairs={{0,2},{2,4},{4,6},{6,8},{8,10},{10,12},{12,14},{14,16},{16,18},{18... | collective-permute-start | bytes 23048 | tf_op jit(solution)/shard_map/ppermute | solution.py:28
  4.8 24.4 %all-to-all-start = ((f32[16,40,1]{1,2,0:T(1,128)}), f32[16,40,1]{1,2,0:T(1,128)S(1)}, u32[]{:S(2)}, u32[]{:S(2)}) async-start(f32[16,40,1]{1,2,0:T(1,128)} %bitcast.2), calls=%async_computation | async-start | bytes 16384 | tf_op jit(solution)/shard_map/all_to_all | solution.py:165
  15.9 0.7 copy-start.1
  15.9 3.2 copy-start.2
  29.2 30.0 %all-to-all-start.1 = ((f32[16,1,40,360]{3,2,1,0:T(8,128)}), f32[16,1,40,360]{3,2,1,0:T(8,128)S(1)}, u32[]{:S(2)}, u32[]{:S(2)}) async-start(f32[16,1,40,360]{3,2,1,0:T(8,128)} %constant_dynamic-update-slice_fusion.2), calls=%async_computation.1 | async-start | bytes 1966080 | tf_op jit(solution)/shard_map/all_to_all | solution.py:162
  37.9 89.0 %collective-permute-start.2 = (f32[5,1,360,2]{2,3,1,0:T(2,128)S(1)}, f32[5,1,360,2]{2,3,1,0:T(2,128)S(1)}, u32[]{:S(2)}, u32[]{:S(2)}) collective-permute-start(f32[5,1,360,2]{2,3,1,0:T(2,128)S(1)} %copy.215), channel_id=1, source_target_pairs={{0,16},{2,18},{4,20},{6,22},{8,24},{10,26},{12,28},{14,30},{16,0},... | collective-permute-start | bytes 43208 | tf_op jit(solution)/shard_map/ppermute | solution.py:18
  43.1 84.7 %collective-permute-start.3 = (f32[5,1,360,3]{2,1,3,0:T(1,128)S(1)}, f32[5,1,360,3]{2,1,3,0:T(1,128)S(1)}, u32[]{:S(2)}, u32[]{:S(2)}) collective-permute-start(f32[5,1,360,3]{2,1,3,0:T(1,128)S(1)} %copy.269), channel_id=1, source_target_pairs={{1,0},{3,2},{5,4},{7,6},{9,8},{11,10},{13,12},{15,14},{17,16},{19,... | collective-permute-start | bytes 64808 | tf_op jit(solution)/shard_map/ppermute | solution.py:29
  45.9 83.2 %collective-permute-start.4 = (f32[5,1,360,3]{2,1,3,0:T(1,128)S(1)}, f32[5,1,360,3]{2,1,3,0:T(1,128)S(1)}, u32[]{:S(2)}, u32[]{:S(2)}) collective-permute-start(f32[5,1,360,3]{2,1,3,0:T(1,128)S(1)} %copy.270), channel_id=1, source_target_pairs={{0,1},{2,3},{4,5},{6,7},{8,9},{10,11},{12,13},{14,15},{16,17},{18,... | collective-permute-start | bytes 64808 | tf_op jit(solution)/shard_map/ppermute | solution.py:28
  121.6 5.3 %copy-start.4 = (f32[5]{0:T(128)S(1)}, f32[5]{0:T(128)}, u32[]{:S(2)}) copy-start(f32[5]{0:T(128)} %constant.123.clone) | copy-start | bytes 64
  121.6 27.7 %all-to-all-start.2 = ((f32[16,1,14400]{2,1,0:T(1,128)}), f32[16,1,14400]{2,1,0:T(1,128)}, u32[]{:S(2)}, u32[]{:S(2)}) async-start(f32[16,1,14400]{2,1,0:T(1,128)} %reshape.644), calls=%async_computation.2 | async-start | bytes 1851392 | tf_op jit(solution)/shard_map/all_to_all | solution.py:167
  170.2 1.0 copy-start.3
  171.6 3.2 collective-permute-start.5
  171.6 3.1 collective-permute-start.6
  188.5 33.8 %all-to-all-start.3 = ((f32[16,1,40,360]{3,2,1,0:T(8,128)}), f32[16,1,40,360]{3,2,1,0:T(8,128)S(1)}, u32[]{:S(2)}, u32[]{:S(2)}) async-start(f32[16,1,40,360]{3,2,1,0:T(8,128)} %constant_dynamic-update-slice_fusion.18), calls=%async_computation.3 | async-start | bytes 1966080 | tf_op jit(solution)/shard_map/all_to_all | solution.py:162
  201.3 90.2 %collective-permute-start.8 = (f32[5,1,360,3]{2,1,3,0:T(1,128)S(1)}, f32[5,1,360,3]{2,1,3,0:T(1,128)S(1)}, u32[]{:S(2)}, u32[]{:S(2)}) collective-permute-start(f32[5,1,360,3]{2,1,3,0:T(1,128)S(1)} %copy.241), channel_id=1, source_target_pairs={{1,0},{3,2},{5,4},{7,6},{9,8},{11,10},{13,12},{15,14},{17,16},{19,... | collective-permute-start | bytes 64808 | tf_op jit(solution)/shard_map/ppermute | solution.py:29
  204.1 88.7 %collective-permute-start.9 = (f32[5,1,360,3]{2,1,3,0:T(1,128)S(1)}, f32[5,1,360,3]{2,1,3,0:T(1,128)S(1)}, u32[]{:S(2)}, u32[]{:S(2)}) collective-permute-start(f32[5,1,360,3]{2,1,3,0:T(1,128)S(1)} %copy.244), channel_id=1, source_target_pairs={{0,1},{2,3},{4,5},{6,7},{8,9},{10,11},{12,13},{14,15},{16,17},{18,... | collective-permute-start | bytes 64808 | tf_op jit(solution)/shard_map/ppermute | solution.py:28
  210.8 78.0 %collective-permute-start.7 = (f32[5,1,360,2]{2,3,1,0:T(2,128)S(1)}, f32[5,1,360,2]{2,3,1,0:T(2,128)S(1)}, u32[]{:S(2)}, u32[]{:S(2)}) collective-permute-start(f32[5,1,360,2]{2,3,1,0:T(2,128)S(1)} %copy.237), channel_id=1, source_target_pairs={{0,16},{2,18},{4,20},{6,22},{8,24},{10,26},{12,28},{14,30},{16,0},... | collective-permute-start | bytes 43208 | tf_op jit(solution)/shard_map/ppermute | solution.py:18
  283.8 27.5 %all-to-all-start.4 = ((f32[16,1,14400]{2,1,0:T(1,128)}), f32[16,1,14400]{2,1,0:T(1,128)S(1)}, u32[]{:S(2)}, u32[]{:S(2)}) async-start(f32[16,1,14400]{2,1,0:T(1,128)} %reshape.646), calls=%async_computation.4 | async-start | bytes 1851392 | tf_op jit(solution)/shard_map/all_to_all | solution.py:167
